TPU v7x, 512 devices: a whole 4x8x8 slice. The times are simulated.
512 devices in a mesh: band: 64 (over z, x, core), mem: 8 (over y).
Axes of the slice: x: 4, y: 8, z: 8, core: 2. Of those that a mesh axis runs over, the one named last changes fastest.
Arguments:
- spectra: bfloat16 [16, 4, 2, 2, 901120], P('mem', None, None, None, 'band'), may hold values from -6 to 6
- legendre: bfloat16 [40, 901120], P(None, 'band'), may hold values from -0.0034179688 to 0.0034179688
- pair_waves: int32 [640], P('band'), may hold values from 0 to 639, each once
- band_lengths: int32 [64], replicated, may hold values from 1 to 2, 80 in all
- eof_basis: bfloat16 [128, 2560, 256], P('band'), may hold values from -0.0390625 to 0.0390625
Outputs:
- grid_fields: bfloat16 [16, 4, 2, 128, 2560], P('mem', None, None, 'band')
- eof_coeffs: float32 [16, 4, 2, 256], P('mem', None, None, 'band')
Inputs may be any that keep to these rules, and one draw needn't show every extreme that they name: `pair_waves`: every lower wavenumber 0 .. 639 stands in exactly one pair slot. `band_lengths`: the lengths sum to 80; some band has exactly 2 rows.
All inputs are finite; a program needn't handle non-finite values.
Results may differ from a plain program's by a relative error of at most 0.0055.
Values may be sent and summed in bfloat16 or wider, within the bound.
No kernel may reach another device: no remote copies, remote signals or barrier semaphores. Data moves between devices by JAX's collectives and lax.ppermute only.
A program may use at most 192 MiB of HBM per device.

v0:
```python
import math
import jax
import jax.numpy as jnp
from jax import lax
from jax.sharding import PartitionSpec as P

WAVE_COUNT = 1280
BLK = 128


def wave_block(orders, start, width, length):
    lon_index = start + jnp.arange(width, dtype=jnp.int32)
    phase_idx = orders[..., None] * lon_index % length
    angle_rad = phase_idx.astype(jnp.float32) * (2.0 * math.pi / length)
    weight = jnp.where(orders == 0, 1.0, 2.0).astype(jnp.float32)[..., None]
    return jnp.stack([weight * jnp.cos(angle_rad), -weight * jnp.sin(angle_rad)]).astype(
        jnp.bfloat16
    )


def shards(spectra, legendre, pair_waves, band_lengths, eof_basis):
    ens_dev, fields, level_stack, re_im, slot_count = spectra.shape
    lat_half = legendre.shape[0]
    pairs_dev = pair_waves.shape[0]
    blocks = slot_count // (pairs_dev * BLK)
    columns = ens_dev * fields * level_stack * re_im
    band_count = lax.axis_size("band")
    most_rows, longitudes, eof_modes = eof_basis.shape
    spectral_data = spectra.reshape(columns, pairs_dev, blocks, BLK)
    legendre_rows = legendre.reshape(lat_half, pairs_dev, blocks, BLK)
    position = jnp.arange(blocks * BLK, dtype=jnp.int32).reshape(1, blocks, BLK)
    lower_wave = pair_waves.reshape(pairs_dev, 1, 1)
    low_blocks = WAVE_COUNT // BLK - lower_wave // BLK
    upper_pos = position - low_blocks * BLK
    in_range = (position < WAVE_COUNT - lower_wave) | (upper_pos >= 0) & (
        upper_pos < lower_wave + 1
    )
    spectral_data = spectral_data * in_range.astype(jnp.bfloat16)[None]
    block_index = jnp.arange(blocks, dtype=jnp.int32)[None, :]
    low_owner = (block_index < low_blocks[:, :, 0]).astype(jnp.float32)
    owners = jnp.stack([low_owner, 1.0 - low_owner], axis=1)
    alternate = jnp.where(jnp.arange(BLK) % 2 == 0, 1.0, -1.0).astype(jnp.bfloat16)
    north_part = jnp.einsum(
        "cptk,jptk->ptcj", spectral_data, legendre_rows, preferred_element_type=jnp.float32
    )
    south_part = jnp.einsum(
        "cptk,jptk->ptcj",
        spectral_data,
        legendre_rows * alternate,
        preferred_element_type=jnp.float32,
    )
    rows_all = jnp.concatenate([north_part, south_part[..., ::-1]], axis=-1)
    fourier = jnp.einsum(
        "pht,ptcj->jphc", owners, rows_all, precision=lax.Precision.HIGHEST
    ).astype(jnp.bfloat16)
    starts = jnp.cumsum(band_lengths) - band_lengths
    offsets = jnp.arange(most_rows, dtype=jnp.int32)
    row_index = jnp.minimum(starts[:, None] + offsets[None, :], 2 * lat_half - 1).reshape(-1)
    packed = jnp.take(fourier, row_index, axis=0).reshape(
        band_count, most_rows, pairs_dev * 2 * columns
    )
    arrived = lax.all_to_all(packed, "band", split_axis=0, concat_axis=0, tiled=True)
    all_waves = lax.all_gather(pair_waves, "band", axis=0, tiled=True).reshape(
        band_count, pairs_dev
    )
    lower_all = all_waves.T
    orders = jnp.stack([lower_all, WAVE_COUNT - 1 - lower_all], axis=1)
    arrived = arrived.reshape(
        band_count, most_rows, pairs_dev, 2, ens_dev, fields, level_stack, re_im
    )
    lon_width = math.gcd(longitudes, 512)
    lon_blocks = longitudes // lon_width

    def synth_block(block_number):
        table_part = wave_block(orders, block_number * lon_width, lon_width, longitudes)
        return jnp.einsum(
            "srphabdc,cphsk->abdrk", arrived, table_part, preferred_element_type=jnp.float32
        )

    grid_parts = lax.map(synth_block, jnp.arange(lon_blocks, dtype=jnp.int32))
    grid_sum = jnp.moveaxis(grid_parts, 0, 4).reshape(
        ens_dev, fields, level_stack, most_rows, longitudes
    )
    own_rows = band_lengths[lax.axis_index("band")]
    row_keep = (offsets < own_rows).astype(jnp.float32)
    grid_fields = (grid_sum * row_keep[:, None]).astype(jnp.bfloat16)
    flat_grid = grid_fields.reshape(ens_dev * fields * level_stack, most_rows * longitudes)
    partial_value = jnp.dot(
        flat_grid,
        eof_basis.reshape(most_rows * longitudes, eof_modes),
        preferred_element_type=jnp.float32,
    )
    share_width = eof_modes // band_count
    summed_all = lax.psum(partial_value, "band")
    own_share = lax.dynamic_slice_in_dim(
        summed_all, lax.axis_index("band") * share_width, share_width, 1
    )
    local_share = own_share.reshape(ens_dev, fields * level_stack, share_width)
    summed = lax.psum(jnp.sum(local_share, axis=0), "mem")
    anomaly = local_share - summed / (ens_dev * lax.axis_size("mem"))
    return (grid_fields, anomaly.reshape(ens_dev, fields, level_stack, share_width))


def solution(mesh):
    return jax.shard_map(
        shards,
        mesh=mesh,
        in_specs=(
            P("mem", None, None, None, "band"),
            P(None, "band"),
            P("band"),
            P(),
            P("band", None, None),
        ),
        out_specs=(P("mem", None, None, "band", None), P("mem", None, None, "band")),
        check_vma=False,
    )
```

profile of v0, /device:TPU:8, one launch (start us, length us, event | category | flops | bytes accessed | tf_op | source)
XLA Modules:
  0.0 406.1 jit_solution(17721014867123769294)
XLA Ops:
  0.7 0.8 broadcast_subtract_fusion.2
  1.5 0.1 broadcast_subtract_fusion.1
  1.6 0.1 compare_convert_fusion
  1.7 0.7 copy.36
  2.4 0.1 reduce-window.9
  2.5 0.1 reduce
  2.6 0.7 sub.62
  3.3 2.6 reshape.297
  5.9 3.4 reshape.301
  9.3 0.1 fusion.26
  9.4 1.5 broadcast_multiply_fusion.1
  10.9 0.2 copy-done.1
  11.1 0.1 broadcast_multiply_fusion
  11.2 2.0 fusion.20
  13.2 2.0 fusion.18
  15.2 4.0 rev.3
  19.2 2.6 pad_maximum_fusion
  21.8 3.3 fusion.15
  25.1 0.4 copy.44
  25.5 0.1 copy.43
  25.6 0.1 min.22
  25.8 2.7 gather_fusion
  28.5 1.8 gather.7
  30.2 0.1 copy.37
  30.4 0.9 broadcast_select_fusion
  31.3 13.8 %all-to-all-start = ((bf16[64,2,640]{2,1,0:T(2,128)(2,1)}), bf16[64,2,640]{2,1,0:T(2,128)(2,1)S(1)}, u32[]{:S(2)}, u32[]{:S(2)}) async-start(bf16[64,2,640]{2,1,0:T(2,128)(2,1)} %broadcast_select_fusion), calls=%async_computation | async-start | bytes 327680 | tf_op jit(solution)/shard_map/all_to_all | solution.py:62
  45.1 1.3 dynamic-slice
  47.1 0.2 dynamic-update-slice
  47.4 20.9 %all-reduce = s32[640]{0:T(1024)S(1)} all-reduce(s32[640]{0:T(1024)S(1)} %dynamic-update-slice), channel_id=1, replica_groups=mesh['band'=64,'mem'=8] {'band'}, use_global_device_ids=true, to_apply=%add | all-reduce | flops 640 | bytes 5120
  68.3 0.1 reshape.294
  68.4 0.1 copy.35
  68.6 0.7 dynamic_slice.13
  69.3 0.7 compare_convert_fusion.1
  70.0 0.3 copy.45
  70.3 0.8 copy.47
  71.1 68.8 %while.12 = (s32[]{:T(128)}, f32[5,2,4,2,2,512]{5,2,3,1,4,0:T(4,128)S(1)}, s32[10,2,64]{2,0,1:T(8,128)S(1)}, s32[5]{0:T(128)S(1)}, bf16[64,2,10,2,2,4,2,2]{0,5,2,3,7,6,4,1:T(4,128)(2,1)}, /*index=5*/s32[]{:T(128)}, s32[1]{0:T(128)}) while((s32[]{:T(128)}, f32[5,2,4,2,2,512]{5,2,3,1,4,0:T(4,128)S(1)}, s32[10,2,64]{2,0,1:T(8,128)S(1)}, ...), condition=%wide.region_2.3_spmd, body=%wide.region_1.2_spmd.sunk | while | flops 97652992 | bytes 6326409 | solution.py:80
  71.1 0.6 dynamic_slice.17
  72.4 11.9 %multiply_convert_fusion.5 = (bf16[1,10,2,64,512]{4,3,1,2,0:T(8,128)(2,1)S(1)}, bf16[1,10,2,64,512]{4,3,1,2,0:T(8,128)(2,1)S(1)}) fusion(s32[512]{0:T(512)S(1)} %iota_add_fusion.2, s32[10,2,64]{2,0,1:T(8,128)S(1)} %get-tuple-element.159, f32[10,2,64]{2,0,1:T(8,128)S(1)} %get-tuple-element.139, f32[10,2,64]{2,0,1:T(8,128)S(1)} %get-tuple-element.140), kind=kLoop, calls=%fused_computation.6.clone.1 | loop fusion | flops 8519680 | bytes 2638848 | tf_op jit(solution)/shard_map/convert
  84.3 0.6 fusion.42
  84.9 0.6 dynamic_slice.17
  86.1 11.9 %multiply_convert_fusion.5 = (bf16[1,10,2,64,512]{4,3,1,2,0:T(8,128)(2,1)S(1)}, bf16[1,10,2,64,512]{4,3,1,2,0:T(8,128)(2,1)S(1)}) fusion(s32[512]{0:T(512)S(1)} %iota_add_fusion.2, s32[10,2,64]{2,0,1:T(8,128)S(1)} %get-tuple-element.159, f32[10,2,64]{2,0,1:T(8,128)S(1)} %get-tuple-element.139, f32[10,2,64]{2,0,1:T(8,128)S(1)} %get-tuple-element.140), kind=kLoop, calls=%fused_computation.6.clone.1 | loop fusion | flops 8519680 | bytes 2638848 | tf_op jit(solution)/shard_map/convert
  98.0 0.6 fusion.42
  98.6 0.6 dynamic_slice.17
  99.9 11.9 %multiply_convert_fusion.5 = (bf16[1,10,2,64,512]{4,3,1,2,0:T(8,128)(2,1)S(1)}, bf16[1,10,2,64,512]{4,3,1,2,0:T(8,128)(2,1)S(1)}) fusion(s32[512]{0:T(512)S(1)} %iota_add_fusion.2, s32[10,2,64]{2,0,1:T(8,128)S(1)} %get-tuple-element.159, f32[10,2,64]{2,0,1:T(8,128)S(1)} %get-tuple-element.139, f32[10,2,64]{2,0,1:T(8,128)S(1)} %get-tuple-element.140), kind=kLoop, calls=%fused_computation.6.clone.1 | loop fusion | flops 8519680 | bytes 2638848 | tf_op jit(solution)/shard_map/convert
  111.8 0.6 fusion.42
  112.4 0.6 dynamic_slice.17
  113.7 11.9 %multiply_convert_fusion.5 = (bf16[1,10,2,64,512]{4,3,1,2,0:T(8,128)(2,1)S(1)}, bf16[1,10,2,64,512]{4,3,1,2,0:T(8,128)(2,1)S(1)}) fusion(s32[512]{0:T(512)S(1)} %iota_add_fusion.2, s32[10,2,64]{2,0,1:T(8,128)S(1)} %get-tuple-element.159, f32[10,2,64]{2,0,1:T(8,128)S(1)} %get-tuple-element.139, f32[10,2,64]{2,0,1:T(8,128)S(1)} %get-tuple-element.140), kind=kLoop, calls=%fused_computation.6.clone.1 | loop fusion | flops 8519680 | bytes 2638848 | tf_op jit(solution)/shard_map/convert
  125.6 0.6 fusion.42
  126.2 0.6 dynamic_slice.17
  127.4 11.9 %multiply_convert_fusion.5 = (bf16[1,10,2,64,512]{4,3,1,2,0:T(8,128)(2,1)S(1)}, bf16[1,10,2,64,512]{4,3,1,2,0:T(8,128)(2,1)S(1)}) fusion(s32[512]{0:T(512)S(1)} %iota_add_fusion.2, s32[10,2,64]{2,0,1:T(8,128)S(1)} %get-tuple-element.159, f32[10,2,64]{2,0,1:T(8,128)S(1)} %get-tuple-element.139, f32[10,2,64]{2,0,1:T(8,128)S(1)} %get-tuple-element.140), kind=kLoop, calls=%fused_computation.6.clone.1 | loop fusion | flops 8519680 | bytes 2638848 | tf_op jit(solution)/shard_map/convert
  139.3 0.6 fusion.42
  139.9 0.1 multiply_convert_fusion.2
  140.1 0.1 copy.49
  140.2 0.2 convert_element_type.82
  140.4 1.1 fusion.35
  141.5 246.2 %psum.14 = f32[16,256]{0,1:T(8,128)S(1)} all-reduce(f32[16,256]{0,1:T(8,128)S(1)} %fusion.35), channel_id=1, replica_groups=mesh['band'=64,'mem'=8] {'band'}, use_global_device_ids=true, to_apply=%region_3.4 | all-reduce | flops 4096 | bytes 32768 | tf_op jit(solution)/shard_map/psum | solution.py:94
  387.7 0.1 reshape.306
  387.8 0.1 copy.50
  387.9 16.2 %psum.15 = f32[8,4]{0,1:T(4,128)S(1)} all-reduce(f32[8,4]{0,1:T(4,128)S(1)} %reduce_sum.9), channel_id=1, replica_groups=mesh['band'=64,'mem'=8] {'mem'}, use_global_device_ids=true, to_apply=%region_5.6 | all-reduce | flops 32 | bytes 256 | tf_op jit(solution)/shard_map/psum | solution.py:99
  404.1 0.1 copy.51
  404.1 0.2 copy.48
  404.4 0.3 reshape.303
  404.6 0.8 multiply_convert_fusion.3
  405.5 0.6 broadcast_subtract_fusion
  (44 shorter events, 0.3 us)
Async XLA Ops:
  0.6 139.7 %copy-start = (bf16[2,2560,256]{2,1,0:T(8,128)(2,1)S(1)}, bf16[2,2560,256]{2,1,0:T(8,128)(2,1)}, u32[]{:S(2)}) copy-start(bf16[2,2560,256]{2,1,0:T(8,128)(2,1)} %param.11) | copy-start | bytes 7864324
  9.3 1.8 copy-start.1
  25.0 22.1 %copy-start.4 = (s32[10]{0:T(128)S(1)}, s32[10]{0:T(128)}, u32[]{:S(2)}) copy-start(s32[10]{0:T(128)} %param.9) | copy-start | bytes 124
  25.1 43.6 %copy-start.3 = (s32[64]{0:T(128)S(1)}, s32[64]{0:T(128)}, u32[]{:S(2)}) copy-start(s32[64]{0:T(128)} %param.10) | copy-start | bytes 772
  31.3 38.7 %all-to-all-start = ((bf16[64,2,640]{2,1,0:T(2,128)(2,1)}), bf16[64,2,640]{2,1,0:T(2,128)(2,1)S(1)}, u32[]{:S(2)}, u32[]{:S(2)}) async-start(bf16[64,2,640]{2,1,0:T(2,128)(2,1)} %broadcast_select_fusion), calls=%async_computation | async-start | bytes 327680 | tf_op jit(solution)/shard_map/all_to_all | solution.py:62
  71.1 13.2 %copy-start.2 = (bf16[64,2,10,2,2,4,2,2]{0,5,2,3,7,6,4,1:T(4,128)(2,1)S(1)}, bf16[64,2,10,2,2,4,2,2]{0,5,2,3,7,6,4,1:T(4,128)(2,1)}, u32[]{:S(2)}) copy-start(bf16[64,2,10,2,2,4,2,2]{0,5,2,3,7,6,4,1:T(4,128)(2,1)} %get-tuple-element.161) | copy-start | bytes 491524 | tf_op jit(solution)/shard_map/while
  84.9 13.2 %copy-start.2 = (bf16[64,2,10,2,2,4,2,2]{0,5,2,3,7,6,4,1:T(4,128)(2,1)S(1)}, bf16[64,2,10,2,2,4,2,2]{0,5,2,3,7,6,4,1:T(4,128)(2,1)}, u32[]{:S(2)}) copy-start(bf16[64,2,10,2,2,4,2,2]{0,5,2,3,7,6,4,1:T(4,128)(2,1)} %get-tuple-element.161) | copy-start | bytes 491524 | tf_op jit(solution)/shard_map/while
  98.6 13.2 %copy-start.2 = (bf16[64,2,10,2,2,4,2,2]{0,5,2,3,7,6,4,1:T(4,128)(2,1)S(1)}, bf16[64,2,10,2,2,4,2,2]{0,5,2,3,7,6,4,1:T(4,128)(2,1)}, u32[]{:S(2)}) copy-start(bf16[64,2,10,2,2,4,2,2]{0,5,2,3,7,6,4,1:T(4,128)(2,1)} %get-tuple-element.161) | copy-start | bytes 491524 | tf_op jit(solution)/shard_map/while
  112.4 13.2 %copy-start.2 = (bf16[64,2,10,2,2,4,2,2]{0,5,2,3,7,6,4,1:T(4,128)(2,1)S(1)}, bf16[64,2,10,2,2,4,2,2]{0,5,2,3,7,6,4,1:T(4,128)(2,1)}, u32[]{:S(2)}) copy-start(bf16[64,2,10,2,2,4,2,2]{0,5,2,3,7,6,4,1:T(4,128)(2,1)} %get-tuple-element.161) | copy-start | bytes 491524 | tf_op jit(solution)/shard_map/while
  126.2 13.2 %copy-start.2 = (bf16[64,2,10,2,2,4,2,2]{0,5,2,3,7,6,4,1:T(4,128)(2,1)S(1)}, bf16[64,2,10,2,2,4,2,2]{0,5,2,3,7,6,4,1:T(4,128)(2,1)}, u32[]{:S(2)}) copy-start(bf16[64,2,10,2,2,4,2,2]{0,5,2,3,7,6,4,1:T(4,128)(2,1)} %get-tuple-element.161) | copy-start | bytes 491524 | tf_op jit(solution)/shard_map/while
where the time goes:
time: 407 us; the launch traced here: 406 us
  blocking collectives  283 us (70%)
  other arithmetic  68.9 us (17%)
  local copies, waits for them, and re-layouts  23.8 us (6%)
  starting transfers between devices  13.8 us (3%)
  matrix products  11.2 us (3%)
    psum x1, blocking collectives, shards(): summed_all = lax.psum(partial_value, 'band')  246 us
    another operation x7, other arithmetic  59.7 us
    unnamed x1, blocking collectives  20.9 us
    psum x1, blocking collectives, shards(): summed = lax.psum(jnp.sum(local_share, axis=0), 'mem')  16.2 us
    all_to_all x1, starting transfers between devices, shards(): lax.all_to_all(packed, 'band', split_axis=0, concat_axis=0, tiled=True)  13.8 us
  transfers between devices with their start and end apart: 1, of which 0 were waited for; matrix products, arithmetic and copies ran while one was open for 1% of the time, Pallas kernels for 0%

commit v1 on v0

--- a/solution.py
+++ b/solution.py
@@ -91,7 +91,8 @@
         preferred_element_type=jnp.float32,
     )
     share_width = eof_modes // band_count
-    summed_all = lax.psum(partial_value, "band")
+    parts = lax.all_gather(partial_value, "band")
+    summed_all = jnp.sum(parts, axis=0)
     own_share = lax.dynamic_slice_in_dim(
         summed_all, lax.axis_index("band") * share_width, share_width, 1
     )

time: 407 us -> 253 us (0.62)
  the two profiles are of different devices: /device:TPU:8 before, /device:TPU:2 now
where the time goes in v1:
time: 253 us; the launch traced here: 252 us
  waiting for transfers between devices  78.2 us (31%)
  other arithmetic  70.3 us (28%)
  blocking collectives  36.5 us (14%)
  local copies, waits for them, and re-layouts  23.6 us (9%)
  between operations  14.9 us (6%)
  starting transfers between devices  13.9 us (5%)
  matrix products  11.1 us (4%)
  loops' own time  3.53 us (1%)
    all_gather x1, waiting for transfers between devices, shards(): parts = lax.all_gather(partial_value, 'band')  78.2 us
    another operation x7, other arithmetic  59.7 us
    unnamed x1, blocking collectives  19.6 us
    psum x1, blocking collectives, shards(): summed = lax.psum(jnp.sum(local_share, axis=0), 'mem')  17 us
    all_to_all x1, starting transfers between devices, shards(): lax.all_to_all(packed, 'band', split_axis=0, concat_axis=0, tiled=True)  13.9 us
  transfers between devices with their start and end apart: 2, of which 1 were waited for; matrix products, arithmetic and copies ran while one was open for 2% of the time, Pallas kernels for 0%

profile of v1, /device:TPU:2, one launch (start us, length us, event | category | flops | bytes accessed | tf_op | source)
XLA Modules:
  0.0 252.2 jit_solution(6456985666413343002)
XLA Ops:
  7.2 0.8 broadcast_subtract_fusion.2
  8.0 0.1 broadcast_subtract_fusion.1
  8.1 0.1 compare_convert_fusion
  8.2 0.7 copy.36
  8.9 0.1 reduce-window.9
  9.0 0.1 reduce
  9.1 0.7 sub.62
  9.8 2.6 %reshape.297 = bf16[32,10,11,128]{3,2,1,0:T(8,128)(2,1)} reshape(bf16[2,4,2,2,14080]{4,3,2,1,0:T(2,128)(2,1)} %param.7) | data formatting | bytes 1802240 | tf_op jit(solution)/shard_map/reshape | solution.py:29
  12.4 3.4 %reshape.301 = bf16[40,10,11,128]{3,2,1,0:T(8,128)(2,1)} reshape(bf16[40,14080]{1,0:T(8,128)(2,1)} %param.8) | data formatting | bytes 2252800 | tf_op jit(solution)/shard_map/reshape | solution.py:30
  15.8 0.1 fusion.26
  15.9 1.5 broadcast_multiply_fusion.1
  17.4 0.2 copy-done.1
  17.6 0.1 broadcast_multiply_fusion
  17.8 2.0 fusion.20
  19.8 2.0 fusion.18
  21.8 4.0 %rev.3 = f32[10,11,32,40]{3,2,1,0:T(8,128)} reverse(f32[10,11,32,40]{3,2,1,0:T(8,128)} %fusion.18), dimensions={3} | reverse | bytes 1126400 | tf_op jit(solution)/shard_map/rev | solution.py:52
  25.7 2.6 %pad_maximum_fusion = f32[10,11,32,80]{3,2,1,0:T(8,128)S(1)} fusion(f32[10,11,32,40]{3,2,1,0:T(8,128)} %rev.3, f32[10,11,32,40]{3,2,1,0:T(8,128)} %fusion.20), kind=kLoop, calls=%fused_computation.20 | loop fusion | flops 281600 | bytes 2252800 | tf_op jit(solution)/shard_map/concatenate | solution.py:52
  28.3 3.3 %fusion.15 = bf16[80,10,2,32]{0,2,3,1:T(2,128)(2,1)S(1)} fusion(f32[10,11,32,80]{3,2,1,0:T(8,128)S(1)} %pad_maximum_fusion, f32[10,1,11]{2,1,0:T(1,128)S(1)} %broadcast_subtract_fusion.1, f32[10,1,11]{2,1,0:T(1,128)S(1)} %compare_convert_fusion), kind=kOutput, calls=%fused_computation.22 | convolution fusion | flops 6809820 | bytes 1229680 | tf_op jit(solution)/shard_map/pht,ptcj->jphc/dot_general | solution.py:53
  31.6 0.4 copy.44
  32.0 0.1 copy.43
  32.1 0.1 min.22
  32.3 2.7 %gather_fusion = bf16[128,10,2,32]{3,2,1,0:T(2,128)(2,1)} fusion(bf16[80,10,2,32]{3,2,1,0:T(2,128)(2,1)S(1)} %copy.44, s32[1024]{0:T(1024)S(1)} %pad_clamp_fusion), kind=kCustom, calls=%fused_computation | custom fusion | bytes 328192 | tf_op jit(solution)/shard_map/jit(_take)/gather | solution.py:59
  35.0 1.8 gather.7
  36.8 0.1 copy.37
  36.9 0.9 broadcast_select_fusion
  37.8 13.9 %all-to-all-start = ((bf16[64,2,640]{2,1,0:T(2,128)(2,1)}), bf16[64,2,640]{2,1,0:T(2,128)(2,1)S(1)}, u32[]{:S(2)}, u32[]{:S(2)}) async-start(bf16[64,2,640]{2,1,0:T(2,128)(2,1)} %broadcast_select_fusion), calls=%async_computation | async-start | bytes 327680 | tf_op jit(solution)/shard_map/all_to_all | solution.py:62
  51.7 1.3 dynamic-slice
  53.7 0.2 dynamic-update-slice
  53.9 19.6 %all-reduce = s32[640]{0:T(1024)S(1)} all-reduce(s32[640]{0:T(1024)S(1)} %dynamic-update-slice), channel_id=1, replica_groups=mesh['band'=64,'mem'=8] {'band'}, use_global_device_ids=true, to_apply=%add | all-reduce | flops 640 | bytes 5120
  73.5 0.1 reshape.294
  73.8 0.7 dynamic_slice.13
  74.5 0.7 compare_convert_fusion.1
  75.2 0.3 copy.45
  75.5 0.8 copy.47
  76.3 68.8 %while.12 = (s32[]{:T(128)}, f32[5,2,4,2,2,512]{5,2,3,1,4,0:T(4,128)S(1)}, s32[10,2,64]{2,0,1:T(8,128)S(1)}, s32[5]{0:T(128)S(1)}, bf16[64,2,10,2,2,4,2,2]{0,5,2,3,7,6,4,1:T(4,128)(2,1)}, /*index=5*/s32[]{:T(128)}, s32[1]{0:T(128)}) while((s32[]{:T(128)}, f32[5,2,4,2,2,512]{5,2,3,1,4,0:T(4,128)S(1)}, s32[10,2,64]{2,0,1:T(8,128)S(1)}, ...), condition=%wide.region_2.3_spmd, body=%wide.region_1.2_spmd.sunk | while | flops 97652992 | bytes 6326409 | solution.py:80
  76.3 0.6 dynamic_slice.18
  77.6 11.9 %multiply_convert_fusion.5 = (bf16[1,10,2,64,512]{4,3,1,2,0:T(8,128)(2,1)S(1)}, bf16[1,10,2,64,512]{4,3,1,2,0:T(8,128)(2,1)S(1)}) fusion(s32[512]{0:T(512)S(1)} %iota_add_fusion.2, s32[10,2,64]{2,0,1:T(8,128)S(1)} %get-tuple-element.161, f32[10,2,64]{2,0,1:T(8,128)S(1)} %get-tuple-element.141, f32[10,2,64]{2,0,1:T(8,128)S(1)} %get-tuple-element.142), kind=kLoop, calls=%fused_computation.6.clone.1 | loop fusion | flops 8519680 | bytes 2638848 | tf_op jit(solution)/shard_map/convert
  89.5 0.6 fusion.42
  90.1 0.6 dynamic_slice.18
  91.4 11.9 %multiply_convert_fusion.5 = (bf16[1,10,2,64,512]{4,3,1,2,0:T(8,128)(2,1)S(1)}, bf16[1,10,2,64,512]{4,3,1,2,0:T(8,128)(2,1)S(1)}) fusion(s32[512]{0:T(512)S(1)} %iota_add_fusion.2, s32[10,2,64]{2,0,1:T(8,128)S(1)} %get-tuple-element.161, f32[10,2,64]{2,0,1:T(8,128)S(1)} %get-tuple-element.141, f32[10,2,64]{2,0,1:T(8,128)S(1)} %get-tuple-element.142), kind=kLoop, calls=%fused_computation.6.clone.1 | loop fusion | flops 8519680 | bytes 2638848 | tf_op jit(solution)/shard_map/convert
  103.3 0.6 fusion.42
  103.8 0.6 dynamic_slice.18
  105.1 11.9 %multiply_convert_fusion.5 = (bf16[1,10,2,64,512]{4,3,1,2,0:T(8,128)(2,1)S(1)}, bf16[1,10,2,64,512]{4,3,1,2,0:T(8,128)(2,1)S(1)}) fusion(s32[512]{0:T(512)S(1)} %iota_add_fusion.2, s32[10,2,64]{2,0,1:T(8,128)S(1)} %get-tuple-element.161, f32[10,2,64]{2,0,1:T(8,128)S(1)} %get-tuple-element.141, f32[10,2,64]{2,0,1:T(8,128)S(1)} %get-tuple-element.142), kind=kLoop, calls=%fused_computation.6.clone.1 | loop fusion | flops 8519680 | bytes 2638848 | tf_op jit(solution)/shard_map/convert
  117.0 0.6 fusion.42
  117.6 0.6 dynamic_slice.18
  118.9 11.9 %multiply_convert_fusion.5 = (bf16[1,10,2,64,512]{4,3,1,2,0:T(8,128)(2,1)S(1)}, bf16[1,10,2,64,512]{4,3,1,2,0:T(8,128)(2,1)S(1)}) fusion(s32[512]{0:T(512)S(1)} %iota_add_fusion.2, s32[10,2,64]{2,0,1:T(8,128)S(1)} %get-tuple-element.161, f32[10,2,64]{2,0,1:T(8,128)S(1)} %get-tuple-element.141, f32[10,2,64]{2,0,1:T(8,128)S(1)} %get-tuple-element.142), kind=kLoop, calls=%fused_computation.6.clone.1 | loop fusion | flops 8519680 | bytes 2638848 | tf_op jit(solution)/shard_map/convert
  130.8 0.6 fusion.42
  131.4 0.6 dynamic_slice.18
  132.6 11.9 %multiply_convert_fusion.5 = (bf16[1,10,2,64,512]{4,3,1,2,0:T(8,128)(2,1)S(1)}, bf16[1,10,2,64,512]{4,3,1,2,0:T(8,128)(2,1)S(1)}) fusion(s32[512]{0:T(512)S(1)} %iota_add_fusion.2, s32[10,2,64]{2,0,1:T(8,128)S(1)} %get-tuple-element.161, f32[10,2,64]{2,0,1:T(8,128)S(1)} %get-tuple-element.141, f32[10,2,64]{2,0,1:T(8,128)S(1)} %get-tuple-element.142), kind=kLoop, calls=%fused_computation.6.clone.1 | loop fusion | flops 8519680 | bytes 2638848 | tf_op jit(solution)/shard_map/convert
  144.5 0.6 fusion.42
  145.1 0.1 multiply_convert_fusion.2
  145.2 0.1 copy.49
  145.4 0.2 convert_element_type.82
  145.6 1.1 fusion.35
  146.7 0.2 copy.48
  146.9 0.3 reshape.303
  147.1 0.8 multiply_convert_fusion.3
  148.0 78.2 %all-gather.3.cloned.1.call-done = f32[1024,256]{1,0:T(8,128)} async-done(((f32[16,256]{1,0:T(8,128)}), f32[1024,256]{1,0:T(8,128)}) %all-gather.3.cloned.1.call-update) | async-done | bytes 1048592 | tf_op jit(solution)/shard_map/all_gather | solution.py:94
  226.2 1.3 reduce_sum.18
  227.5 0.1 bitcast_reduce_fusion
  227.6 0.1 copy.56
  227.7 17.0 %psum.7 = f32[8,4]{0,1:T(4,128)S(1)} all-reduce(f32[8,4]{0,1:T(4,128)S(1)} %copy.56), channel_id=1, replica_groups=mesh['band'=64,'mem'=8] {'mem'}, use_global_device_ids=true, to_apply=%region_5.6 | all-reduce | flops 32 | bytes 256 | tf_op jit(solution)/shard_map/psum | solution.py:100
  244.6 0.1 copy.51
  244.7 0.6 broadcast_subtract_fusion
  (45 shorter events, 0.4 us)
Async XLA Ops:
  7.2 138.4 %copy-start = (bf16[2,2560,256]{2,1,0:T(8,128)(2,1)S(1)}, bf16[2,2560,256]{2,1,0:T(8,128)(2,1)}, u32[]{:S(2)}) copy-start(bf16[2,2560,256]{2,1,0:T(8,128)(2,1)} %param.11) | copy-start | bytes 7864324
  15.8 1.8 copy-start.1
  31.6 22.1 %copy-start.4 = (s32[10]{0:T(128)S(1)}, s32[10]{0:T(128)}, u32[]{:S(2)}) copy-start(s32[10]{0:T(128)} %param.9) | copy-start | bytes 124
  31.6 42.2 %copy-start.3 = (s32[64]{0:T(128)S(1)}, s32[64]{0:T(128)}, u32[]{:S(2)}) copy-start(s32[64]{0:T(128)} %param.10) | copy-start | bytes 772
  37.8 37.4 %all-to-all-start = ((bf16[64,2,640]{2,1,0:T(2,128)(2,1)}), bf16[64,2,640]{2,1,0:T(2,128)(2,1)S(1)}, u32[]{:S(2)}, u32[]{:S(2)}) async-start(bf16[64,2,640]{2,1,0:T(2,128)(2,1)} %broadcast_select_fusion), calls=%async_computation | async-start | bytes 327680 | tf_op jit(solution)/shard_map/all_to_all | solution.py:62
  51.7 174.5 %all-gather.3.cloned.1.call-start = ((), (), s32[]{:S(2)}) async-start(), calls=%async_computation.1 | async-start | bytes 1064960 | tf_op jit(solution)/shard_map/all_gather | solution.py:94
  76.3 13.2 %copy-start.2 = (bf16[64,2,10,2,2,4,2,2]{0,5,2,3,7,6,4,1:T(4,128)(2,1)S(1)}, bf16[64,2,10,2,2,4,2,2]{0,5,2,3,7,6,4,1:T(4,128)(2,1)}, u32[]{:S(2)}) copy-start(bf16[64,2,10,2,2,4,2,2]{0,5,2,3,7,6,4,1:T(4,128)(2,1)} %get-tuple-element.163) | copy-start | bytes 491524 | tf_op jit(solution)/shard_map/while
  90.1 13.2 %copy-start.2 = (bf16[64,2,10,2,2,4,2,2]{0,5,2,3,7,6,4,1:T(4,128)(2,1)S(1)}, bf16[64,2,10,2,2,4,2,2]{0,5,2,3,7,6,4,1:T(4,128)(2,1)}, u32[]{:S(2)}) copy-start(bf16[64,2,10,2,2,4,2,2]{0,5,2,3,7,6,4,1:T(4,128)(2,1)} %get-tuple-element.163) | copy-start | bytes 491524 | tf_op jit(solution)/shard_map/while
  103.8 13.2 %copy-start.2 = (bf16[64,2,10,2,2,4,2,2]{0,5,2,3,7,6,4,1:T(4,128)(2,1)S(1)}, bf16[64,2,10,2,2,4,2,2]{0,5,2,3,7,6,4,1:T(4,128)(2,1)}, u32[]{:S(2)}) copy-start(bf16[64,2,10,2,2,4,2,2]{0,5,2,3,7,6,4,1:T(4,128)(2,1)} %get-tuple-element.163) | copy-start | bytes 491524 | tf_op jit(solution)/shard_map/while
  117.6 13.2 %copy-start.2 = (bf16[64,2,10,2,2,4,2,2]{0,5,2,3,7,6,4,1:T(4,128)(2,1)S(1)}, bf16[64,2,10,2,2,4,2,2]{0,5,2,3,7,6,4,1:T(4,128)(2,1)}, u32[]{:S(2)}) copy-start(bf16[64,2,10,2,2,4,2,2]{0,5,2,3,7,6,4,1:T(4,128)(2,1)} %get-tuple-element.163) | copy-start | bytes 491524 | tf_op jit(solution)/shard_map/while
  131.4 13.2 %copy-start.2 = (bf16[64,2,10,2,2,4,2,2]{0,5,2,3,7,6,4,1:T(4,128)(2,1)S(1)}, bf16[64,2,10,2,2,4,2,2]{0,5,2,3,7,6,4,1:T(4,128)(2,1)}, u32[]{:S(2)}) copy-start(bf16[64,2,10,2,2,4,2,2]{0,5,2,3,7,6,4,1:T(4,128)(2,1)} %get-tuple-element.163) | copy-start | bytes 491524 | tf_op jit(solution)/shard_map/while
Sparse Core Ops, SparseCore 0:
  146.8 79.3 all-gather.2
